TPU v7x, 256 devices: a whole 4x4x8 slice. The times are simulated.
256 devices in a mesh: gx: 32 (over z, x_lo, core), gy: 8 (over y, x_hi).
Axes of the slice: x: 4 (x_hi: 2, x_lo: 2; x = x_hi * 2 + x_lo), y: 4, z: 8, core: 2. Of those that a mesh axis runs over, the one named last changes fastest.
Arguments:
- field: float32 [32, 128, 128, 256], P(None, 'gx', 'gy'), may hold values from -6 to 6
- spec_weight: float32 [2, 32, 32, 32, 32, 32], P(None, None, 'gx', 'gy'), may hold values from -6 to 6
- dw_kernel: float32 [32, 3, 3, 3], replicated, may hold values from -1.25 to 1.25
- point_weight: float32 [32, 32], replicated, may hold values from -1 to 1
- bias: float32 [32], replicated, may hold values from -3 to 3
Outputs:
- evolved: float32 [32, 128, 128, 256], P(None, 'gx', 'gy')
All inputs are finite; a program needn't handle non-finite values.
Results may differ from a plain program's by a relative error of at most 0.00005.
Values sent between devices are 32-bit elements; how exact they have to be, the bound alone decides.
No kernel may reach another device: no remote copies, remote signals or barrier semaphores. Data moves between devices by JAX's collectives and lax.ppermute only.
A program may use at most 128 MiB of HBM per device.

v0:
```python
import jax
import jax.numpy as jnp
from jax import lax
from jax.sharding import PartitionSpec as P

full_turn = 6.283185307179586


def extended(array, sides, width):
    for axis, dim in sides:
        count, length = (lax.axis_size(axis), array.shape[dim])
        up = [(i, (i + 1) % count) for i in range(count)]
        down = [(j, i) for i, j in up]
        last = lax.slice_in_dim(array, length - width, length, axis=dim)
        leading = lax.slice_in_dim(array, 0, width, axis=dim)
        before = lax.ppermute(last, axis, up)
        after = lax.ppermute(leading, axis, down)
        array = jnp.concatenate([before, array, after], axis=dim)
    return array


def kept_index(modes, length):
    index = jnp.arange(modes, dtype=jnp.int32)
    return jnp.where(index < modes // 2, index, index + length - modes)


def phase_table(freqs, positions, length):
    product = freqs[:, None] * positions[None, :] % length
    angle = product.astype(jnp.float32) * (full_turn / length)
    return (jnp.cos(angle), jnp.sin(angle))


def complex_table(cosine, sine_tab, direction):
    upper = jnp.stack([cosine, direction * sine_tab])
    lower = jnp.stack([-direction * sine_tab, cosine])
    return jnp.stack([upper, lower])


def on_device(field, spec_weight, dw_kernel, point_weight, bias):
    exact_mode = lax.Precision.HIGHEST
    chans, rows_x, rows_y, depth = field.shape
    modes = spec_weight.shape[1]
    full_x = rows_x * lax.axis_size("gx")
    full_y = rows_y * lax.axis_size("gy")
    zfreqs = jnp.arange(modes, dtype=jnp.int32)
    zcosine, zsine = phase_table(zfreqs, jnp.arange(depth, dtype=jnp.int32), depth)
    forward_z = jnp.concatenate([zcosine, -zsine], axis=0)
    zspec = jnp.einsum("tz,cxyz->tcxy", forward_z, field, precision=exact_mode).reshape(
        2, modes, chans, rows_x, rows_y
    )
    yfreqs = kept_index(modes, full_y)
    wide = lax.all_to_all(zspec, "gy", split_axis=1, concat_axis=4, tiled=True)
    ycosine, ysine = phase_table(yfreqs, jnp.arange(full_y, dtype=jnp.int32), full_y)
    ytable = complex_table(ycosine, ysine, 1.0)
    yspec = jnp.einsum("srny,rkcxy->snxkc", ytable, wide, precision=exact_mode)
    yspec = yspec.reshape(2, modes, rows_x, -1)
    columns = lax.all_to_all(yspec, "gx", split_axis=1, concat_axis=2, tiled=True)
    xcosine, xsine = phase_table(
        kept_index(modes, full_x), jnp.arange(full_x, dtype=jnp.int32), full_x
    )
    xtable = complex_table(xcosine, xsine, 1.0)
    xspec = jnp.einsum("srma,rnak->snmk", xtable, columns, precision=exact_mode)
    cols_loc = xspec.shape[1]
    xin = xspec.reshape(2, cols_loc, modes, -1, chans)
    weight_re = spec_weight[0]
    weight_im = spec_weight[1]
    stacked = jnp.stack([jnp.stack([weight_re, -weight_im]), jnp.stack([weight_im, weight_re])])
    mixed = jnp.einsum("rnmki,srmnkio->snmko", xin, stacked, precision=exact_mode)
    mixed = mixed.reshape(2, cols_loc, modes, -1)
    xinverse = complex_table(xcosine / full_x, xsine / full_x, -1.0)
    back_x = jnp.einsum("srma,rnmk->snak", xinverse, mixed, precision=exact_mode)
    rows_back = lax.all_to_all(back_x, "gx", split_axis=2, concat_axis=1, tiled=True)
    yinverse = complex_table(ycosine / full_y, ysine / full_y, -1.0)
    tall = jnp.einsum("srnb,rnxk->sbxk", yinverse, rows_back, precision=exact_mode)
    zback = lax.all_to_all(tall, "gy", split_axis=1, concat_axis=3, tiled=True)
    weights_z = jnp.where(zfreqs == 0, 1.0, 2.0).astype(jnp.float32)[:, None] / depth
    backward_z = jnp.stack([weights_z * zcosine, -weights_z * zsine])
    zcells = zback.reshape(2, rows_y, rows_x, modes, chans)
    spectral = jnp.einsum("skz,syxkc->cxyz", backward_z, zcells, precision=exact_mode)
    framed = extended(field, (("gx", 1), ("gy", 2)), 1)
    framed = jnp.concatenate([framed[..., -1:], framed, framed[..., :1]], axis=3)
    conv = jnp.zeros(field.shape, jnp.float32)
    for shift_x in range(3):
        for shift_y in range(3):
            for shift_z in range(3):
                tap = dw_kernel[:, shift_x, shift_y, shift_z][:, None, None, None]
                conv = (
                    conv
                    + tap
                    * framed[
                        :,
                        shift_x : shift_x + rows_x,
                        shift_y : shift_y + rows_y,
                        shift_z : shift_z + depth,
                    ]
                )
    pointwise = jnp.dot(point_weight.T, field.reshape(chans, -1), precision=exact_mode).reshape(
        field.shape
    )
    total = spectral + conv + pointwise + bias[:, None, None, None]
    return jax.nn.gelu(total)


def solution(mesh):
    placed = (P(None, "gx", "gy", None), P(None, None, "gx", "gy", None, None), P(), P(), P())
    return jax.shard_map(
        on_device, mesh=mesh, in_specs=placed, out_specs=P(None, "gx", "gy", None), check_vma=False
    )
```

profile of v0, /device:TPU:1, one launch (start us, length us, event | category | flops | bytes accessed | tf_op | source)
XLA Modules:
  0.0 143.8 jit_solution(5653876701960673272)
XLA Ops:
  0.2 4.2 %fusion.61 = f32[64,32,4,16]{0,1,3,2:T(8,128)S(1)} fusion(f32[32,256]{1,0:T(8,128)S(1)} %get-tuple-element.53, f32[32,256]{1,0:T(8,128)S(1)} %get-tuple-element.54, f32[32,4,16,256]{3,2,1,0:T(8,128)} %param.5), kind=kOutput, calls=%fused_computation.102 | convolution fusion | flops 402669568 | bytes 2686976 | tf_op jit(solution)/shard_map/tz,cxyz->tcxy/dot_general | solution.py:48
  4.4 1.2 reshape.378
  5.6 2.9 %copy.48 = f32[2,32,32,4,16]{2,4,3,0,1:T(8,128)} copy(f32[2,32,32,4,16]{1,0,2,4,3:T(2,128)S(1)} %reshape.378) | data formatting | bytes 1048576 | tf_op jit(solution)/shard_map/reshape | solution.py:48
  8.5 3.3 %reshape.404 = f32[8,1,16384]{2,1,0:T(1,128)} reshape(f32[32,2,4,16,32]{4,3,2,1,0:T(8,128)} %bitcast.180) | data formatting | bytes 1048576
  11.8 7.5 %all-to-all-start = ((f32[8,1,16384]{2,1,0:T(1,128)}), f32[8,1,16384]{2,1,0:T(1,128)S(1)}, u32[]{:S(2)}, u32[]{:S(2)}) async-start(f32[8,1,16384]{2,1,0:T(1,128)} %reshape.404), calls=%async_computation | async-start | bytes 1048576 | tf_op jit(solution)/shard_map/all_to_all | solution.py:52
  19.3 1.2 copy.47
  20.5 1.1 fusion.103
  21.6 1.2 collective-permute-start
  22.9 0.3 slice.210
  23.2 1.2 fusion.100
  24.4 0.7 slice_bitcast_fusion.26
  25.0 2.5 %maximum_bitcast_fusion.1 = f32[1,2,32,1,4,32,32]{6,5,4,2,1,3,0:T(8,128)} fusion(f32[1,32,1,4,32,32]{5,4,3,1,0,2:T(8,128)S(1)} %get-tuple-element.52, f32[1,32,1,4,32,32]{5,4,3,1,0,2:T(8,128)S(1)} %get-tuple-element.5), kind=kLoop, calls=%fused_computation.9 | loop fusion | flops 262144 | bytes 2097152 | tf_op jit(solution)/shard_map/stack | solution.py:67
  27.5 2.5 %maximum_bitcast_fusion.2 = f32[1,2,32,1,4,32,32]{6,5,4,2,1,3,0:T(8,128)} fusion(f32[1,32,1,4,32,32]{5,4,3,2,1,0:T(8,128)S(1)} %get-tuple-element.6, f32[1,32,1,4,32,32]{5,4,3,2,1,0:T(8,128)S(1)} %slice.210), kind=kLoop, calls=%fused_computation.10 | loop fusion | flops 262144 | bytes 2097152 | tf_op jit(solution)/shard_map/stack | solution.py:67
  30.0 0.6 maximum_bitcast_fusion.7
  30.7 0.8 sine_multiply_fusion
  31.5 0.6 broadcast.504
  32.0 1.9 %reduce = f32[8,16384]{1,0:T(8,128)S(1)} reduce(f32[8,1,16384]{2,1,0:T(1,128)S(1)} %all-to-all-done, f32[]{:T(128)} %broadcast.504), dimensions={1}, to_apply=%all_to_all.40.reduce_sub_computation | reduce | bytes 1048580 | tf_op jit(solution)/shard_map/all_to_all | solution.py:52
  34.0 2.0 %reshape.405 = f32[32,2,4,16,32]{4,3,2,1,0:T(8,128)} reshape(f32[8,16384]{1,0:T(8,128)S(1)} %reduce) | data formatting | bytes 1048576
  36.0 1.8 %copy.50 = f32[2,4,32,4,8,16]{2,5,4,3,1,0:T(8,128)S(1)} copy(f32[2,4,32,4,8,16]{2,5,3,0,1,4:T(8,128)} %bitcast.181) | data formatting | bytes 1048576 | tf_op jit(solution)/shard_map/all_to_all | solution.py:52
  37.8 3.5 %fusion.55 = f32[2,32,4,4,32]{1,4,0,2,3:T(8,128)S(1)} fusion(f32[2,4,32,4,128,1]{2,4,3,1,0,5:T(8,128)S(1)} %bitcast.182, f32[1,2,32,128]{3,2,1,0:T(8,128)S(1)} %get-tuple-element.55, f32[1,2,32,128]{3,2,1,0:T(8,128)S(1)} %get-tuple-element.56), kind=kOutput, calls=%fused_computation.91 | convolution fusion | flops 100679680 | bytes 720896 | tf_op jit(solution)/shard_map/srny,rkcxy->snxkc/dot_general | solution.py:55
  41.3 0.6 copy.88
  41.9 1.0 reshape.401
  42.8 14.5 %all-to-all-start.1 = ((f32[2,32,4,128]{3,2,0,1:T(4,128)}), f32[2,32,4,128]{3,2,0,1:T(4,128)S(1)}, u32[]{:S(2)}, u32[]{:S(2)}) async-start(f32[2,32,4,128]{3,2,0,1:T(4,128)} %reshape.401), calls=%async_computation.1 | async-start | bytes 262144 | tf_op jit(solution)/shard_map/all_to_all | solution.py:57
  57.3 1.1 constant_dynamic-update-slice_fusion.2
  58.4 1.2 constant_dynamic-update-slice_fusion.1
  59.6 1.1 constant_dynamic-update-slice_fusion
  60.7 1.7 %copy-done.2 = f32[32,6,16,256]{3,0,2,1:T(8,128)} copy-done((f32[32,6,16,256]{3,0,2,1:T(8,128)}, f32[32,6,16,256]{3,0,2,1:T(8,128)S(1)}, u32[]{:S(2)}) %copy-start.2) | copy-done | bytes 3145752
  62.5 1.1 collective-permute-start.2
  63.6 4.0 %collective-permute-start.3 = (f32[32,6,1,256]{3,0,2,1:T(8,128)S(1)}, f32[32,6,1,256]{3,0,2,1:T(8,128)S(1)}, u32[]{:S(2)}, u32[]{:S(2)}) collective-permute-start(f32[32,6,1,256]{3,0,2,1:T(8,128)S(1)} %get-tuple-element.12), channel_id=1, source_target_pairs={{1,0},{2,1},{3,2},{4,3},{5,4},{6,5},{7,6},{0,7},{9,8},{10,9},{11,1... | collective-permute-start | bytes 589832 | tf_op jit(solution)/shard_map/ppermute | solution.py:17
  67.7 0.2 convolution_bitcast_fusion.2
  68.1 7.2 %fusion = f32[32,4,1,2,32,1]{4,2,5,3,1,0:T(1,128)S(1)} fusion(f32[2,32,4,32,1,1]{3,2,1,0,4,5:T(4,128)S(1)} %reshape.391, f32[1,2,32,1,4,32,32]{6,5,4,2,1,3,0:T(8,128)} %maximum_bitcast_fusion.2, f32[1,2,32,1,4,32,32]{6,5,4,2,1,3,0:T(8,128)} %maximum_bitcast_fusion.1), kind=kOutput, calls=%fused_computation.1 | convolution fusion | flops 6815744 | bytes 2162688 | tf_op jit(solution)/shard_map/rnmki,srmnkio->snmko/dot_general | solution.py:68
  75.5 0.3 convolution_bitcast_fusion.1
  75.8 0.8 copy.55
  76.6 8.8 %all-to-all-start.2 = ((f32[2,1,128,128]{3,0,1,2:T(2,128)}), f32[2,1,128,128]{3,0,1,2:T(2,128)S(1)}, u32[]{:S(2)}, u32[]{:S(2)}) async-start(f32[2,1,128,128]{3,0,1,2:T(2,128)} %copy.55), calls=%async_computation.2 | async-start | bytes 262144 | tf_op jit(solution)/shard_map/all_to_all | solution.py:72
  85.4 1.4 slice_bitcast_fusion.25
  86.9 4.1 %pad_maximum_fusion.1 = f32[32,6,18,256]{3,0,2,1:T(8,128)} fusion(f32[32,6,1,256]{3,0,2,1:T(8,128)S(1)} %collective-permute-done.3, f32[32,6,16,256]{3,0,2,1:T(8,128)} %copy-done.2, f32[32,6,1,256]{3,0,2,1:T(8,128)S(1)} %collective-permute-done.2), kind=kLoop, calls=%fused_computation.11 | loop fusion | flops 1769472 | bytes 7077888 | tf_op jit(solution)/shard_map/concatenate | solution.py:18
  91.0 3.7 %all-to-all-done.2 = f32[2,1,128,128]{3,0,1,2:T(2,128)S(1)} async-done(((f32[2,1,128,128]{3,0,1,2:T(2,128)}), f32[2,1,128,128]{3,0,1,2:T(2,128)S(1)}, u32[]{:S(2)}, u32[]{:S(2)}) %all-to-all-start.2) | async-done | bytes 131104 | tf_op jit(solution)/shard_map/all_to_all | solution.py:72
  94.7 0.6 convolution_bitcast_fusion
  95.3 1.2 copy.58
  96.5 3.5 %all-to-all-start.3 = ((f32[2,128,4,128]{3,2,0,1:T(4,128)}), f32[2,128,4,128]{3,2,0,1:T(4,128)S(1)}, u32[]{:S(2)}, u32[]{:S(2)}) async-start(f32[2,128,4,128]{3,2,0,1:T(4,128)} %copy.58), calls=%async_computation.3 | async-start | bytes 1048576 | tf_op jit(solution)/shard_map/all_to_all | solution.py:75
  100.0 2.8 %fusion.101 = (f32[32,6,18,1]{3,0,2,1:T(8,128)S(1)}, f32[32,6,18,1]{3,0,2,1:T(8,128)S(1)}) fusion(f32[32,6,18,256]{3,0,2,1:T(8,128)} %pad_maximum_fusion.1), kind=kLoop, calls=%fused_computation.197 | loop fusion | bytes 55296 | tf_op jit(solution)/shard_map/slice | solution.py:81
  102.9 5.5 %maximum_maximum_fusion = (f32[32,6,18,257]{3,0,2,1:T(8,128)}, f32[32,6,18,257]{3,0,2,1:T(8,128)}) fusion(f32[32,6,1,256]{3,0,2,1:T(8,128)S(1)} %collective-permute-done.3, f32[32,6,16,256]{3,0,2,1:T(8,128)S(1)} %copy-done.3, f32[32,6,1,256]{3,0,2,1:T(8,128)S(1)} %collective-permute-done.2, f32[32,6,18,1]{3,0,2,1:T(8,128)S(1)} %get-tuple-element.9, ...), kind=kLoop, calls=%fused_computation.3 | loop fusion | flops 5329152 | bytes 10672128 | tf_op jit(solution)/shard_map/concatenate | solution.py:81
  108.4 2.3 %all-to-all-done.3 = f32[2,128,4,128]{3,2,0,1:T(4,128)S(1)} async-done(((f32[2,128,4,128]{3,2,0,1:T(4,128)}), f32[2,128,4,128]{3,2,0,1:T(4,128)S(1)}, u32[]{:S(2)}, u32[]{:S(2)}) %all-to-all-start.3) | async-done | bytes 524320 | tf_op jit(solution)/shard_map/all_to_all | solution.py:75
  110.7 0.3 copy.119
  111.0 1.8 %reshape.383 = f32[2,16,4,32,32]{4,3,2,1,0:T(8,128)} reshape(f32[2,16,4,8,128]{4,3,2,1,0:T(8,128)S(1)} %bitcast.183) | data formatting | bytes 1048576 | tf_op jit(solution)/shard_map/reshape | solution.py:78
  113.1 5.3 %fusion.64 = f32[16,4,32,256,1]{3,2,1,0,4:T(8,128)S(1)} fusion(f32[2,16,4,32,32]{4,3,2,1,0:T(8,128)} %reshape.383, f32[1,32,256]{2,1,0:T(8,128)} %get-tuple-element.57, f32[1,32,256]{2,1,0:T(8,128)} %get-tuple-element.58), kind=kOutput, calls=%fused_computation.107 | convolution fusion | flops 402669568 | bytes 2686976 | tf_op jit(solution)/shard_map/skz,syxkc->cxyz/dot_general | solution.py:79
  118.7 22.6 %fusion.8 = f32[32,4,16,256]{3,0,2,1:T(8,128)S(1)} fusion(f32[32,6,18,257]{3,0,2,1:T(8,128)} %get-tuple-element.8, f32[32,6,1,256]{3,0,2,1:T(8,128)S(1)} %collective-permute-done.3, f32[32,6,16,256]{3,0,2,1:T(8,128)S(1)} %copy-done.4, f32[32,6,18,257]{3,0,2,1:T(8,128)} %get-tuple-element.7, f32[32,1,16,256]{3,0,2,1:T(8,128)} %collective-permute-done.1, ...), kind=kOutput, calls=%fused_computation.23 | convolution fusion | flops 239075328 | bytes 50732544 | tf_op jit(solution)/shard_map/dot_general | solution.py:97
  141.3 2.5 %copy.69 = f32[32,4,16,256]{3,2,1,0:T(8,128)} copy(f32[32,4,16,256]{3,0,2,1:T(8,128)S(1)} %fusion.8) | data formatting | bytes 4194304 | tf_op jit(solution)/shard_map/mul | solution.py:101
  (100 shorter events, 1.0 us)
Async XLA Ops:
  0.0 118.4 %copy-start = (f32[32,32]{1,0:T(8,128)S(1)}, f32[32,32]{1,0:T(8,128)}, u32[]{:S(2)}) copy-start(f32[32,32]{1,0:T(8,128)} %param.8) | copy-start | bytes 12292
  8.5 10.7 %copy-start.1 = (f32[32,4,16,256]{3,2,1,0:T(8,128)S(1)}, f32[32,4,16,256]{3,2,1,0:T(8,128)}, u32[]{:S(2)}) copy-start(f32[32,4,16,256]{3,2,1,0:T(8,128)} %param.5) | copy-start | bytes 6291460
  11.8 19.7 %all-to-all-start = ((f32[8,1,16384]{2,1,0:T(1,128)}), f32[8,1,16384]{2,1,0:T(1,128)S(1)}, u32[]{:S(2)}, u32[]{:S(2)}) async-start(f32[8,1,16384]{2,1,0:T(1,128)} %reshape.404), calls=%async_computation | async-start | bytes 1048576 | tf_op jit(solution)/shard_map/all_to_all | solution.py:52
  19.3 3.6 %copy-start.5 = (f32[2,32,1,4,32,32]{5,4,3,2,1,0:T(8,128)S(1)}, f32[2,32,1,4,32,32]{5,4,3,2,1,0:T(8,128)}, u32[]{:S(2)}) copy-start(f32[2,32,1,4,32,32]{5,4,3,2,1,0:T(8,128)} %param.6) | copy-start | bytes 3145732
  20.5 2.7 %copy-start.6 = (f32[32,4,16,256]{3,0,2,1:T(8,128)}, f32[32,4,16,256]{3,0,2,1:T(8,128)S(1)}, u32[]{:S(2)}) copy-start(f32[32,4,16,256]{3,0,2,1:T(8,128)S(1)} %copy.47) | copy-start | bytes 6291460
  21.6 35.7 %collective-permute-start = (f32[32,1,16,256]{3,0,2,1:T(8,128)}, f32[32,1,16,256]{3,0,2,1:T(8,128)}, u32[]{:S(2)}, u32[]{:S(2)}) collective-permute-start(f32[32,1,16,256]{3,0,2,1:T(8,128)} %get-tuple-element.14), channel_id=1, source_target_pairs={{0,8},{8,16},{16,24},{24,32},{32,40},{40,48},{48,56},{56,64},{64,7... | collective-permute-start | bytes 1572872 | tf_op jit(solution)/shard_map/ppermute | solution.py:16
  22.7 36.9 %collective-permute-start.1 = (f32[32,1,16,256]{3,0,2,1:T(8,128)}, f32[32,1,16,256]{3,0,2,1:T(8,128)}, u32[]{:S(2)}, u32[]{:S(2)}) collective-permute-start(f32[32,1,16,256]{3,0,2,1:T(8,128)} %get-tuple-element.13), channel_id=1, source_target_pairs={{8,0},{16,8},{24,16},{32,24},{40,32},{48,40},{56,48},{64,56},{72,6... | collective-permute-start | bytes 1572872 | tf_op jit(solution)/shard_map/ppermute | solution.py:17
  30.7 7.1 %copy-start.7 = (f32[1,2,32,128]{3,2,1,0:T(8,128)}, f32[1,2,32,128]{3,2,1,0:T(8,128)S(1)}, u32[]{:S(2)}) copy-start(f32[1,2,32,128]{3,2,1,0:T(8,128)S(1)} %get-tuple-element.55) | copy-start | bytes 98308
  30.7 7.2 %copy-start.9 = (f32[1,2,32,128]{3,2,1,0:T(8,128)}, f32[1,2,32,128]{3,2,1,0:T(8,128)S(1)}, u32[]{:S(2)}) copy-start(f32[1,2,32,128]{3,2,1,0:T(8,128)S(1)} %get-tuple-element.56) | copy-start | bytes 98308
  42.8 24.8 %all-to-all-start.1 = ((f32[2,32,4,128]{3,2,0,1:T(4,128)}), f32[2,32,4,128]{3,2,0,1:T(4,128)S(1)}, u32[]{:S(2)}, u32[]{:S(2)}) async-start(f32[2,32,4,128]{3,2,0,1:T(4,128)} %reshape.401), calls=%async_computation.1 | async-start | bytes 262144 | tf_op jit(solution)/shard_map/all_to_all | solution.py:57
  59.6 8.1 %copy-start.8 = (f32[1,2,32,128]{3,2,1,0:T(8,128)S(1)}, f32[1,2,32,128]{3,2,1,0:T(8,128)}, u32[]{:S(2)}) copy-start(f32[1,2,32,128]{3,2,1,0:T(8,128)} %copy-done.7) | copy-start | bytes 98308
  59.6 8.1 %copy-start.10 = (f32[1,2,32,128]{3,2,1,0:T(8,128)S(1)}, f32[1,2,32,128]{3,2,1,0:T(8,128)}, u32[]{:S(2)}) copy-start(f32[1,2,32,128]{3,2,1,0:T(8,128)} %copy-done.9) | copy-start | bytes 98308
  62.5 24.3 %collective-permute-start.2 = (f32[32,6,1,256]{3,0,2,1:T(8,128)S(1)}, f32[32,6,1,256]{3,0,2,1:T(8,128)S(1)}, u32[]{:S(2)}, u32[]{:S(2)}) collective-permute-start(f32[32,6,1,256]{3,0,2,1:T(8,128)S(1)} %get-tuple-element.11), channel_id=1, source_target_pairs={{0,1},{1,2},{2,3},{3,4},{4,5},{5,6},{6,7},{7,0},{8,9},{9,10},{10,1... | collective-permute-start | bytes 589832 | tf_op jit(solution)/shard_map/ppermute | solution.py:16
  63.6 23.2 %collective-permute-start.3 = (f32[32,6,1,256]{3,0,2,1:T(8,128)S(1)}, f32[32,6,1,256]{3,0,2,1:T(8,128)S(1)}, u32[]{:S(2)}, u32[]{:S(2)}) collective-permute-start(f32[32,6,1,256]{3,0,2,1:T(8,128)S(1)} %get-tuple-element.12), channel_id=1, source_target_pairs={{1,0},{2,1},{3,2},{4,3},{5,4},{6,5},{7,6},{0,7},{9,8},{10,9},{11,1... | collective-permute-start | bytes 589832 | tf_op jit(solution)/shard_map/ppermute | solution.py:17
  68.0 7.4 %copy-start.11 = (f32[1,2,32,128]{3,2,1,0:T(8,128)S(1)}, f32[1,2,32,128]{3,2,1,0:T(8,128)}, u32[]{:S(2)}) copy-start(f32[1,2,32,128]{3,2,1,0:T(8,128)} %get-tuple-element.42) | copy-start | bytes 98308
  68.1 7.4 %copy-start.12 = (f32[1,2,32,128]{3,2,1,0:T(8,128)S(1)}, f32[1,2,32,128]{3,2,1,0:T(8,128)}, u32[]{:S(2)}) copy-start(f32[1,2,32,128]{3,2,1,0:T(8,128)} %get-tuple-element.43) | copy-start | bytes 98308
  76.6 18.1 %all-to-all-start.2 = ((f32[2,1,128,128]{3,0,1,2:T(2,128)}), f32[2,1,128,128]{3,0,1,2:T(2,128)S(1)}, u32[]{:S(2)}, u32[]{:S(2)}) async-start(f32[2,1,128,128]{3,0,1,2:T(2,128)} %copy.55), calls=%async_computation.2 | async-start | bytes 262144 | tf_op jit(solution)/shard_map/all_to_all | solution.py:72
  96.5 14.2 %all-to-all-start.3 = ((f32[2,128,4,128]{3,2,0,1:T(4,128)}), f32[2,128,4,128]{3,2,0,1:T(4,128)S(1)}, u32[]{:S(2)}, u32[]{:S(2)}) async-start(f32[2,128,4,128]{3,2,0,1:T(4,128)} %copy.58), calls=%async_computation.3 | async-start | bytes 1048576 | tf_op jit(solution)/shard_map/all_to_all | solution.py:75
  100.0 3.0 %copy-start.3 = (f32[32,6,16,256]{3,0,2,1:T(8,128)S(1)}, f32[32,6,16,256]{3,0,2,1:T(8,128)}, u32[]{:S(2)}) copy-start(f32[32,6,16,256]{3,0,2,1:T(8,128)} %copy-done.2) | copy-start | bytes 9437188
  112.8 5.6 %copy-start.4 = (f32[32,6,16,256]{3,0,2,1:T(8,128)S(1)}, f32[32,6,16,256]{3,0,2,1:T(8,128)}, u32[]{:S(2)}) copy-start(f32[32,6,16,256]{3,0,2,1:T(8,128)} %copy-done.2) | copy-start | bytes 9437188
  112.8 5.6 %copy-start.14 = (f32[32]{0:T(128)S(1)}, f32[32]{0:T(128)}, u32[]{:S(2)}) copy-start(f32[32]{0:T(128)} %get-tuple-element.15) | copy-start | bytes 388
  112.8 5.6 %copy-start.15 = (f32[32]{0:T(128)S(1)}, f32[32]{0:T(128)}, u32[]{:S(2)}) copy-start(f32[32]{0:T(128)} %get-tuple-element.16) | copy-start | bytes 388
  112.8 5.6 %copy-start.16 = (f32[32]{0:T(128)S(1)}, f32[32]{0:T(128)}, u32[]{:S(2)}) copy-start(f32[32]{0:T(128)} %get-tuple-element.17) | copy-start | bytes 388
  112.8 5.6 %copy-start.17 = (f32[32]{0:T(128)S(1)}, f32[32]{0:T(128)}, u32[]{:S(2)}) copy-start(f32[32]{0:T(128)} %get-tuple-element.18) | copy-start | bytes 388
  112.8 5.6 %copy-start.18 = (f32[32]{0:T(128)S(1)}, f32[32]{0:T(128)}, u32[]{:S(2)}) copy-start(f32[32]{0:T(128)} %get-tuple-element.19) | copy-start | bytes 388
  112.8 5.6 %copy-start.19 = (f32[32]{0:T(128)S(1)}, f32[32]{0:T(128)}, u32[]{:S(2)}) copy-start(f32[32]{0:T(128)} %get-tuple-element.20) | copy-start | bytes 388
  112.8 5.6 %copy-start.20 = (f32[32]{0:T(128)S(1)}, f32[32]{0:T(128)}, u32[]{:S(2)}) copy-start(f32[32]{0:T(128)} %get-tuple-element.21) | copy-start | bytes 388
  112.9 5.6 %copy-start.21 = (f32[32]{0:T(128)S(1)}, f32[32]{0:T(128)}, u32[]{:S(2)}) copy-start(f32[32]{0:T(128)} %get-tuple-element.22) | copy-start | bytes 388
  112.9 5.6 %copy-start.22 = (f32[32]{0:T(128)S(1)}, f32[32]{0:T(128)}, u32[]{:S(2)}) copy-start(f32[32]{0:T(128)} %get-tuple-element.23) | copy-start | bytes 388
  112.9 5.6 %copy-start.23 = (f32[32]{0:T(128)S(1)}, f32[32]{0:T(128)}, u32[]{:S(2)}) copy-start(f32[32]{0:T(128)} %get-tuple-element.24) | copy-start | bytes 388
  112.9 5.6 %copy-start.24 = (f32[32]{0:T(128)S(1)}, f32[32]{0:T(128)}, u32[]{:S(2)}) copy-start(f32[32]{0:T(128)} %get-tuple-element.25) | copy-start | bytes 388
  112.9 5.6 %copy-start.25 = (f32[32]{0:T(128)S(1)}, f32[32]{0:T(128)}, u32[]{:S(2)}) copy-start(f32[32]{0:T(128)} %get-tuple-element.26) | copy-start | bytes 388
  112.9 5.6 %copy-start.26 = (f32[32]{0:T(128)S(1)}, f32[32]{0:T(128)}, u32[]{:S(2)}) copy-start(f32[32]{0:T(128)} %get-tuple-element.27) | copy-start | bytes 388
  112.9 5.6 %copy-start.27 = (f32[32]{0:T(128)S(1)}, f32[32]{0:T(128)}, u32[]{:S(2)}) copy-start(f32[32]{0:T(128)} %get-tuple-element.28) | copy-start | bytes 388
  112.9 5.6 %copy-start.28 = (f32[32]{0:T(128)S(1)}, f32[32]{0:T(128)}, u32[]{:S(2)}) copy-start(f32[32]{0:T(128)} %get-tuple-element.29) | copy-start | bytes 388
  112.9 5.6 %copy-start.29 = (f32[32]{0:T(128)S(1)}, f32[32]{0:T(128)}, u32[]{:S(2)}) copy-start(f32[32]{0:T(128)} %get-tuple-element.30) | copy-start | bytes 388
  112.9 5.6 %copy-start.30 = (f32[32]{0:T(128)S(1)}, f32[32]{0:T(128)}, u32[]{:S(2)}) copy-start(f32[32]{0:T(128)} %get-tuple-element.31) | copy-start | bytes 388
  113.0 5.6 %copy-start.31 = (f32[32]{0:T(128)S(1)}, f32[32]{0:T(128)}, u32[]{:S(2)}) copy-start(f32[32]{0:T(128)} %get-tuple-element.32) | copy-start | bytes 388
  113.0 5.6 %copy-start.32 = (f32[32]{0:T(128)S(1)}, f32[32]{0:T(128)}, u32[]{:S(2)}) copy-start(f32[32]{0:T(128)} %get-tuple-element.33) | copy-start | bytes 388
  113.0 5.6 %copy-start.33 = (f32[32]{0:T(128)S(1)}, f32[32]{0:T(128)}, u32[]{:S(2)}) copy-start(f32[32]{0:T(128)} %get-tuple-element.34) | copy-start | bytes 388
  113.0 5.6 %copy-start.34 = (f32[32]{0:T(128)S(1)}, f32[32]{0:T(128)}, u32[]{:S(2)}) copy-start(f32[32]{0:T(128)} %get-tuple-element.35) | copy-start | bytes 388
  113.0 5.6 %copy-start.35 = (f32[32]{0:T(128)S(1)}, f32[32]{0:T(128)}, u32[]{:S(2)}) copy-start(f32[32]{0:T(128)} %get-tuple-element.36) | copy-start | bytes 388
  113.0 5.6 %copy-start.36 = (f32[32]{0:T(128)S(1)}, f32[32]{0:T(128)}, u32[]{:S(2)}) copy-start(f32[32]{0:T(128)} %get-tuple-element.37) | copy-start | bytes 388
  113.0 5.6 %copy-start.37 = (f32[32]{0:T(128)S(1)}, f32[32]{0:T(128)}, u32[]{:S(2)}) copy-start(f32[32]{0:T(128)} %get-tuple-element.38) | copy-start | bytes 388
  113.0 5.6 %copy-start.38 = (f32[32]{0:T(128)S(1)}, f32[32]{0:T(128)}, u32[]{:S(2)}) copy-start(f32[32]{0:T(128)} %get-tuple-element.39) | copy-start | bytes 388
  113.0 5.6 %copy-start.39 = (f32[32]{0:T(128)S(1)}, f32[32]{0:T(128)}, u32[]{:S(2)}) copy-start(f32[32]{0:T(128)} %get-tuple-element.40) | copy-start | bytes 388
  113.0 5.6 %copy-start.40 = (f32[32]{0:T(128)S(1)}, f32[32]{0:T(128)}, u32[]{:S(2)}) copy-start(f32[32]{0:T(128)} %get-tuple-element.41) | copy-start | bytes 388
  113.1 5.6 %copy-start.41 = (f32[32]{0:T(128)S(1)}, f32[32]{0:T(128)}, u32[]{:S(2)}) copy-start(f32[32]{0:T(128)} %param.9) | copy-start | bytes 388
  (2 other events, 2.9 us)
where the time goes:
time: 144 us
  matrix products  44 us (31%)
  starting transfers between devices  40.6 us (28%)
  local copies, waits for them, and re-layouts  33 us (23%)
  other arithmetic  19.4 us (13%)
  waiting for transfers between devices  6 us (4%)
    dot_general x1, matrix products, on_device(): jnp.dot(point_weight.T, field.reshape(chans, -1), precision=exact_mode)  22.6 us
    all_to_all x1, starting transfers between devices, on_device(): lax.all_to_all(yspec, 'gx', split_axis=1, concat_axis=2, tiled=True)  14.5 us
    unnamed x89, local copies, waits for them, and re-layouts  10.9 us
    all_to_all x1, starting transfers between devices, on_device(): lax.all_to_all(back_x, 'gx', split_axis=2, concat_axis=1, tiled=True)  8.83 us
    all_to_all x1, starting transfers between devices, on_device(): wide = lax.all_to_all(zspec, 'gy', split_axis=1, concat_axis=4, tiled=True)  7.48 us
    dot_general x1, matrix products, on_device(): jnp.einsum('rnmki,srmnkio->snmko', xin, stacked, precision=exact_mode)  7.24 us
    concatenate x1, other arithmetic, on_device(): jnp.concatenate([framed[..., -1:], framed, framed[..., :1]], axis=3)  5.5 us
    dot_general x1, matrix products, on_device(): jnp.einsum('skz,syxkc->cxyz', backward_z, zcells, precision=exact_mode)  5.29 us
  transfers between devices with their start and end apart: 8, of which 2 were waited for; matrix products, arithmetic and copies ran while one was open for 34% of the time, Pallas kernels for 0%

commit v1 on v0

--- a/solution.py
+++ b/solution.py
@@ -49,7 +49,9 @@
         2, modes, chans, rows_x, rows_y
     )
     yfreqs = kept_index(modes, full_y)
-    wide = lax.all_to_all(zspec, "gy", split_axis=1, concat_axis=4, tiled=True)
+    wide = jnp.concatenate(
+        lax.all_to_all(jnp.stack(jnp.split(zspec, lax.axis_size("gy"), axis=1)), "gy", 0, 0), axis=4
+    )
     ycosine, ysine = phase_table(yfreqs, jnp.arange(full_y, dtype=jnp.int32), full_y)
     ytable = complex_table(ycosine, ysine, 1.0)
     yspec = jnp.einsum("srny,rkcxy->snxkc", ytable, wide, precision=exact_mode)

time: 144 us -> 148 us (1.028)
  local copies, waits for them, and re-layouts: 33 us -> 37.7 us
    unnamed x89 -> x98, local copies, waits for them, and re-layouts: 10.9 us -> 15.8 us
    reshape x2 -> x1, local copies, waits for them, and re-layouts: 4.11 us -> 1.91 us  [on_device(): jnp.einsum('tz,cxyz->tcxy', forward_z, field, precision=exact_mode)]
    reshape x0 -> x2, local copies, waits for them, and re-layouts: none -> 2 us  [on_device(): jnp.concatenate(lax.all_to_all(jnp.stack(jnp.split(zspec, lax.axis_size('...]
    another operation x2 -> x3, local copies, waits for them, and re-layouts: 0.23 us -> 2.05 us  [the longest x1 1.82 us: on_device(): jnp.stack(jnp.split(zspec, lax.axis_size('gy'), axis=1))]
    all_to_all x2 -> x1, local copies, waits for them, and re-layouts: 2.41 us -> 0.61 us  [on_device(): lax.all_to_all(jnp.stack(jnp.split(zspec, lax.axis_size('gy'), axis=1)),...]
  transfers between devices with their start and end apart: 8 -> 8, of which waited for: 2 -> 2; matrix products, arithmetic and copies ran while one was open for 34% -> 33% of each run, Pallas kernels for 0% -> 0%
where the time goes in v1:
time: 148 us
  matrix products  43.1 us (29%)
  starting transfers between devices  40.6 us (27%)
  local copies, waits for them, and re-layouts  37.7 us (25%)
  other arithmetic  19.4 us (13%)
  waiting for transfers between devices  6.02 us (4%)
    dot_general x1, matrix products, on_device(): jnp.dot(point_weight.T, field.reshape(chans, -1), precision=exact_mode)  21.7 us
    unnamed x98, local copies, waits for them, and re-layouts  15.8 us
    all_to_all x1, starting transfers between devices, on_device(): lax.all_to_all(yspec, 'gx', split_axis=1, concat_axis=2, tiled=True)  14.4 us
    all_to_all x1, starting transfers between devices, on_device(): lax.all_to_all(back_x, 'gx', split_axis=2, concat_axis=1, tiled=True)  8.83 us
    all_to_all x1, starting transfers between devices, on_device(): lax.all_to_all(jnp.stack(jnp.split(zspec, lax.axis_size('gy'), axis=1)),...  7.48 us
    dot_general x1, matrix products, on_device(): jnp.einsum('rnmki,srmnkio->snmko', xin, stacked, precision=exact_mode)  7.24 us
    concatenate x1, other arithmetic, on_device(): jnp.concatenate([framed[..., -1:], framed, framed[..., :1]], axis=3)  5.49 us
    dot_general x1, matrix products, on_device(): jnp.einsum('skz,syxkc->cxyz', backward_z, zcells, precision=exact_mode)  5.29 us
  transfers between devices with their start and end apart: 8, of which 2 were waited for; matrix products, arithmetic and copies ran while one was open for 33% of the time, Pallas kernels for 0%

profile of v1, /device:TPU:1, one launch (start us, length us, event | category | flops | bytes accessed | tf_op | source)
XLA Modules:
  0.0 147.6 jit_solution(14081820207444335215)
XLA Ops:
  0.2 4.2 %fusion.69 = f32[64,32,4,16]{0,1,3,2:T(8,128)S(1)} fusion(f32[32,256]{1,0:T(8,128)S(1)} %get-tuple-element.53, f32[32,256]{1,0:T(8,128)S(1)} %get-tuple-element.54, f32[32,4,16,256]{3,2,1,0:T(8,128)} %param.5), kind=kOutput, calls=%fused_computation.118 | convolution fusion | flops 402669568 | bytes 2686976 | tf_op jit(solution)/shard_map/tz,cxyz->tcxy/dot_general | solution.py:48
  4.4 1.9 %copy.103 = f32[64,32,4,16]{1,3,2,0:T(8,128)S(1)} copy(f32[64,32,4,16]{0,1,3,2:T(8,128)S(1)} %fusion.69) | data formatting | bytes 1048576 | tf_op jit(solution)/shard_map/reshape | solution.py:48
  6.3 0.8 fusion.65
  7.1 0.8 fusion.64
  7.8 0.7 fusion.63
  8.6 0.7 fusion.62
  9.3 0.7 fusion.61
  10.0 0.7 fusion.60
  10.7 0.7 fusion.59
  11.4 1.8 %fusion.58 = f32[8,2,4,32,4,16]{3,5,4,2,1,0:T(8,128)} fusion(f32[8,2,4,32,4,16]{3,5,4,2,1,0:T(8,128)} %fusion.59, f32[2,32,32,4,16]{2,4,3,1,0:T(8,128)} %bitcast.216), kind=kLoop, calls=%fused_computation.97 | loop fusion | bytes 524288 | tf_op jit(solution)/shard_map/stack | solution.py:53
  13.3 3.1 %reshape.412 = f32[8,1,16384]{2,1,0:T(1,128)} reshape(f32[8,2,4,4,16,32]{5,4,3,2,1,0:T(8,128)} %bitcast.196) | data formatting | bytes 1048576
  16.4 7.5 %all-to-all-start = ((f32[8,1,16384]{2,1,0:T(1,128)}), f32[8,1,16384]{2,1,0:T(1,128)S(1)}, u32[]{:S(2)}, u32[]{:S(2)}) async-start(f32[8,1,16384]{2,1,0:T(1,128)} %reshape.412), calls=%async_computation | async-start | bytes 1048576 | tf_op jit(solution)/shard_map/all_to_all | solution.py:53
  23.9 1.2 copy.53
  25.1 1.0 fusion.111
  26.2 1.2 collective-permute-start
  27.6 1.2 fusion.108
  28.8 0.7 slice_bitcast_fusion.34
  29.5 2.5 %maximum_bitcast_fusion.1 = f32[1,2,32,1,4,32,32]{6,5,4,2,1,3,0:T(8,128)} fusion(f32[1,32,1,4,32,32]{5,4,3,1,0,2:T(8,128)S(1)} %get-tuple-element.52, f32[1,32,1,4,32,32]{5,4,3,1,0,2:T(8,128)S(1)} %get-tuple-element.5), kind=kLoop, calls=%fused_computation.9 | loop fusion | flops 262144 | bytes 2097152 | tf_op jit(solution)/shard_map/stack | solution.py:69
  31.9 0.8 sine_multiply_fusion
  32.7 2.5 %maximum_bitcast_fusion.2 = f32[1,2,32,1,4,32,32]{6,5,4,2,1,3,0:T(8,128)} fusion(f32[1,32,1,4,32,32]{5,4,3,2,1,0:T(8,128)S(1)} %get-tuple-element.6, f32[1,32,1,4,32,32]{5,4,3,2,1,0:T(8,128)S(1)} %slice.210), kind=kLoop, calls=%fused_computation.10 | loop fusion | flops 262144 | bytes 2097152 | tf_op jit(solution)/shard_map/stack | solution.py:69
  35.4 0.6 maximum_bitcast_fusion.7
  36.7 1.9 %reduce = f32[8,16384]{1,0:T(8,128)S(1)} reduce(f32[8,1,16384]{2,1,0:T(1,128)S(1)} %all-to-all-done, f32[]{:T(128)} %broadcast.504), dimensions={1}, to_apply=%all_to_all.14.reduce_sub_computation | reduce | bytes 1048580 | tf_op jit(solution)/shard_map/all_to_all | solution.py:53
  38.6 2.0 %reshape.413 = f32[8,2,4,4,16,32]{5,4,3,2,1,0:T(8,128)} reshape(f32[8,16384]{1,0:T(8,128)S(1)} %reduce) | data formatting | bytes 1048576
  40.6 1.7 %bitcast_bitcast_fusion = f32[2,4,32,4,8,16]{2,5,3,1,0,4:T(8,128)S(1)} fusion(f32[8,2,4,4,16,32]{5,4,3,2,1,0:T(8,128)} %reshape.413), kind=kLoop, calls=%fused_computation.216 | loop fusion | bytes 1048576 | tf_op jit(solution)/shard_map/reshape | solution.py:52
  42.6 3.5 %fusion.55 = f32[2,32,4,4,32]{1,4,0,2,3:T(8,128)S(1)} fusion(f32[2,4,32,4,128,1]{2,4,3,1,0,5:T(8,128)S(1)} %bitcast.217, f32[1,2,32,128]{3,2,1,0:T(8,128)S(1)} %get-tuple-element.55, f32[1,2,32,128]{3,2,1,0:T(8,128)S(1)} %get-tuple-element.56), kind=kOutput, calls=%fused_computation.91 | convolution fusion | flops 100679680 | bytes 720896 | tf_op jit(solution)/shard_map/srny,rkcxy->snxkc/dot_general | solution.py:57
  46.7 0.9 reshape.409
  47.6 14.4 %all-to-all-start.1 = ((f32[2,32,4,128]{3,2,0,1:T(4,128)}), f32[2,32,4,128]{3,2,0,1:T(4,128)S(1)}, u32[]{:S(2)}, u32[]{:S(2)}) async-start(f32[2,32,4,128]{3,2,0,1:T(4,128)} %reshape.409), calls=%async_computation.1 | async-start | bytes 262144 | tf_op jit(solution)/shard_map/all_to_all | solution.py:59
  62.1 1.1 constant_dynamic-update-slice_fusion.2
  63.2 1.2 constant_dynamic-update-slice_fusion.1
  64.4 1.1 constant_dynamic-update-slice_fusion
  65.5 1.7 %copy-done.2 = f32[32,6,16,256]{3,0,2,1:T(8,128)} copy-done((f32[32,6,16,256]{3,0,2,1:T(8,128)}, f32[32,6,16,256]{3,0,2,1:T(8,128)S(1)}, u32[]{:S(2)}) %copy-start.2) | copy-done | bytes 3145752
  67.3 1.1 collective-permute-start.2
  68.4 4.0 %collective-permute-start.3 = (f32[32,6,1,256]{3,0,2,1:T(8,128)S(1)}, f32[32,6,1,256]{3,0,2,1:T(8,128)S(1)}, u32[]{:S(2)}, u32[]{:S(2)}) collective-permute-start(f32[32,6,1,256]{3,0,2,1:T(8,128)S(1)} %get-tuple-element.12), channel_id=1, source_target_pairs={{1,0},{2,1},{3,2},{4,3},{5,4},{6,5},{7,6},{0,7},{9,8},{10,9},{11,1... | collective-permute-start | bytes 589832 | tf_op jit(solution)/shard_map/ppermute | solution.py:17
  72.8 7.2 %fusion = f32[32,4,1,2,32,1]{4,2,5,3,1,0:T(1,128)S(1)} fusion(f32[2,32,4,32,1,1]{3,2,1,0,4,5:T(4,128)S(1)} %reshape.399, f32[1,2,32,1,4,32,32]{6,5,4,2,1,3,0:T(8,128)} %maximum_bitcast_fusion.2, f32[1,2,32,1,4,32,32]{6,5,4,2,1,3,0:T(8,128)} %maximum_bitcast_fusion.1), kind=kOutput, calls=%fused_computation.1 | convolution fusion | flops 6815744 | bytes 2162688 | tf_op jit(solution)/shard_map/rnmki,srmnkio->snmko/dot_general | solution.py:70
  80.6 0.8 copy.67
  81.3 8.8 %all-to-all-start.2 = ((f32[2,1,128,128]{3,0,1,2:T(2,128)}), f32[2,1,128,128]{3,0,1,2:T(2,128)S(1)}, u32[]{:S(2)}, u32[]{:S(2)}) async-start(f32[2,1,128,128]{3,0,1,2:T(2,128)} %copy.67), calls=%async_computation.2 | async-start | bytes 262144 | tf_op jit(solution)/shard_map/all_to_all | solution.py:74
  90.2 1.4 slice_bitcast_fusion.33
  91.6 4.1 %pad_maximum_fusion.1 = f32[32,6,18,256]{3,0,2,1:T(8,128)} fusion(f32[32,6,1,256]{3,0,2,1:T(8,128)S(1)} %collective-permute-done.3, f32[32,6,16,256]{3,0,2,1:T(8,128)} %copy-done.2, f32[32,6,1,256]{3,0,2,1:T(8,128)S(1)} %collective-permute-done.2), kind=kLoop, calls=%fused_computation.11 | loop fusion | flops 1769472 | bytes 7077888 | tf_op jit(solution)/shard_map/concatenate | solution.py:18
  95.7 3.7 %all-to-all-done.2 = f32[2,1,128,128]{3,0,1,2:T(2,128)S(1)} async-done(((f32[2,1,128,128]{3,0,1,2:T(2,128)}), f32[2,1,128,128]{3,0,1,2:T(2,128)S(1)}, u32[]{:S(2)}, u32[]{:S(2)}) %all-to-all-start.2) | async-done | bytes 131104 | tf_op jit(solution)/shard_map/all_to_all | solution.py:74
  100.1 1.1 copy.70
  101.2 3.5 %all-to-all-start.3 = ((f32[2,128,4,128]{3,2,0,1:T(4,128)}), f32[2,128,4,128]{3,2,0,1:T(4,128)S(1)}, u32[]{:S(2)}, u32[]{:S(2)}) async-start(f32[2,128,4,128]{3,2,0,1:T(4,128)} %copy.70), calls=%async_computation.3 | async-start | bytes 1048576 | tf_op jit(solution)/shard_map/all_to_all | solution.py:77
  104.7 2.8 %fusion.109 = (f32[32,6,18,1]{3,0,2,1:T(8,128)S(1)}, f32[32,6,18,1]{3,0,2,1:T(8,128)S(1)}) fusion(f32[32,6,18,256]{3,0,2,1:T(8,128)} %pad_maximum_fusion.1), kind=kLoop, calls=%fused_computation.213 | loop fusion | bytes 55296 | tf_op jit(solution)/shard_map/slice | solution.py:83
  107.7 5.5 %maximum_maximum_fusion = (f32[32,6,18,257]{3,0,2,1:T(8,128)}, f32[32,6,18,257]{3,0,2,1:T(8,128)}) fusion(f32[32,6,1,256]{3,0,2,1:T(8,128)S(1)} %collective-permute-done.3, f32[32,6,16,256]{3,0,2,1:T(8,128)S(1)} %copy-done.3, f32[32,6,1,256]{3,0,2,1:T(8,128)S(1)} %collective-permute-done.2, f32[32,6,18,1]{3,0,2,1:T(8,128)S(1)} %get-tuple-element.9, ...), kind=kLoop, calls=%fused_computation.3 | loop fusion | flops 5329152 | bytes 10672128 | tf_op jit(solution)/shard_map/concatenate | solution.py:83
  113.2 2.3 %all-to-all-done.3 = f32[2,128,4,128]{3,2,0,1:T(4,128)S(1)} async-done(((f32[2,128,4,128]{3,2,0,1:T(4,128)}), f32[2,128,4,128]{3,2,0,1:T(4,128)S(1)}, u32[]{:S(2)}, u32[]{:S(2)}) %all-to-all-start.3) | async-done | bytes 524320 | tf_op jit(solution)/shard_map/all_to_all | solution.py:77
  115.8 1.8 %reshape.391 = f32[2,16,4,32,32]{4,3,2,1,0:T(8,128)} reshape(f32[2,16,4,8,128]{4,3,2,1,0:T(8,128)S(1)} %bitcast.218) | data formatting | bytes 1048576 | tf_op jit(solution)/shard_map/reshape | solution.py:80
  117.8 5.3 %fusion.72 = f32[16,4,32,256,1]{3,2,1,0,4:T(8,128)S(1)} fusion(f32[2,16,4,32,32]{4,3,2,1,0:T(8,128)} %reshape.391, f32[1,32,256]{2,1,0:T(8,128)} %get-tuple-element.57, f32[1,32,256]{2,1,0:T(8,128)} %get-tuple-element.58), kind=kOutput, calls=%fused_computation.123 | convolution fusion | flops 402669568 | bytes 2686976 | tf_op jit(solution)/shard_map/skz,syxkc->cxyz/dot_general | solution.py:81
  123.4 21.7 %fusion.8 = f32[32,4,16,256]{3,0,2,1:T(8,128)S(1)} fusion(f32[32,6,18,257]{3,0,2,1:T(8,128)} %get-tuple-element.8, f32[32,6,1,256]{3,0,2,1:T(8,128)S(1)} %collective-permute-done.3, f32[32,6,16,256]{3,0,2,1:T(8,128)S(1)} %copy-done.4, f32[32,6,18,257]{3,0,2,1:T(8,128)} %get-tuple-element.7, f32[32,1,16,256]{3,0,2,1:T(8,128)} %collective-permute-done.1, ...), kind=kOutput, calls=%fused_computation.23 | convolution fusion | flops 239075328 | bytes 50732544 | tf_op jit(solution)/shard_map/dot_general | solution.py:99
  145.1 2.5 %copy.81 = f32[32,4,16,256]{3,2,1,0:T(8,128)} copy(f32[32,4,16,256]{3,0,2,1:T(8,128)S(1)} %fusion.8) | data formatting | bytes 4194304 | tf_op jit(solution)/shard_map/mul | solution.py:103
  (110 shorter events, 4.2 us)
Async XLA Ops:
  0.0 123.1 %copy-start = (f32[32,32]{1,0:T(8,128)S(1)}, f32[32,32]{1,0:T(8,128)}, u32[]{:S(2)}) copy-start(f32[32,32]{1,0:T(8,128)} %param.8) | copy-start | bytes 12292
  6.3 4.4 %copy-start.6 = (f32[64,32,4,16]{1,3,2,0:T(8,128)}, f32[64,32,4,16]{1,3,2,0:T(8,128)S(1)}, u32[]{:S(2)}) copy-start(f32[64,32,4,16]{1,3,2,0:T(8,128)S(1)} %copy.103) | copy-start | bytes 1572868
  11.4 12.4 %copy-start.1 = (f32[32,4,16,256]{3,2,1,0:T(8,128)S(1)}, f32[32,4,16,256]{3,2,1,0:T(8,128)}, u32[]{:S(2)}) copy-start(f32[32,4,16,256]{3,2,1,0:T(8,128)} %param.5) | copy-start | bytes 6291460
  16.4 19.7 %all-to-all-start = ((f32[8,1,16384]{2,1,0:T(1,128)}), f32[8,1,16384]{2,1,0:T(1,128)S(1)}, u32[]{:S(2)}, u32[]{:S(2)}) async-start(f32[8,1,16384]{2,1,0:T(1,128)} %reshape.412), calls=%async_computation | async-start | bytes 1048576 | tf_op jit(solution)/shard_map/all_to_all | solution.py:53
  23.9 3.5 %copy-start.5 = (f32[2,32,1,4,32,32]{5,4,3,2,1,0:T(8,128)S(1)}, f32[2,32,1,4,32,32]{5,4,3,2,1,0:T(8,128)}, u32[]{:S(2)}) copy-start(f32[2,32,1,4,32,32]{5,4,3,2,1,0:T(8,128)} %param.6) | copy-start | bytes 3145732
  26.2 35.9 %collective-permute-start = (f32[32,1,16,256]{3,0,2,1:T(8,128)}, f32[32,1,16,256]{3,0,2,1:T(8,128)}, u32[]{:S(2)}, u32[]{:S(2)}) collective-permute-start(f32[32,1,16,256]{3,0,2,1:T(8,128)} %get-tuple-element.14), channel_id=1, source_target_pairs={{0,8},{8,16},{16,24},{24,32},{32,40},{40,48},{48,56},{56,64},{64,7... | collective-permute-start | bytes 1572872 | tf_op jit(solution)/shard_map/ppermute | solution.py:16
  27.3 37.1 %collective-permute-start.1 = (f32[32,1,16,256]{3,0,2,1:T(8,128)}, f32[32,1,16,256]{3,0,2,1:T(8,128)}, u32[]{:S(2)}, u32[]{:S(2)}) collective-permute-start(f32[32,1,16,256]{3,0,2,1:T(8,128)} %get-tuple-element.13), channel_id=1, source_target_pairs={{8,0},{16,8},{24,16},{32,24},{40,32},{48,40},{56,48},{64,56},{72,6... | collective-permute-start | bytes 1572872 | tf_op jit(solution)/shard_map/ppermute | solution.py:17
  36.0 6.6 %copy-start.8 = (f32[1,2,32,128]{3,2,1,0:T(8,128)}, f32[1,2,32,128]{3,2,1,0:T(8,128)S(1)}, u32[]{:S(2)}) copy-start(f32[1,2,32,128]{3,2,1,0:T(8,128)S(1)} %get-tuple-element.55) | copy-start | bytes 98308
  36.0 6.6 %copy-start.10 = (f32[1,2,32,128]{3,2,1,0:T(8,128)}, f32[1,2,32,128]{3,2,1,0:T(8,128)S(1)}, u32[]{:S(2)}) copy-start(f32[1,2,32,128]{3,2,1,0:T(8,128)S(1)} %get-tuple-element.56) | copy-start | bytes 98308
  47.6 24.8 %all-to-all-start.1 = ((f32[2,32,4,128]{3,2,0,1:T(4,128)}), f32[2,32,4,128]{3,2,0,1:T(4,128)S(1)}, u32[]{:S(2)}, u32[]{:S(2)}) async-start(f32[2,32,4,128]{3,2,0,1:T(4,128)} %reshape.409), calls=%async_computation.1 | async-start | bytes 262144 | tf_op jit(solution)/shard_map/all_to_all | solution.py:59
  64.4 8.1 %copy-start.9 = (f32[1,2,32,128]{3,2,1,0:T(8,128)S(1)}, f32[1,2,32,128]{3,2,1,0:T(8,128)}, u32[]{:S(2)}) copy-start(f32[1,2,32,128]{3,2,1,0:T(8,128)} %copy-done.8) | copy-start | bytes 98308
  64.4 8.1 %copy-start.11 = (f32[1,2,32,128]{3,2,1,0:T(8,128)S(1)}, f32[1,2,32,128]{3,2,1,0:T(8,128)}, u32[]{:S(2)}) copy-start(f32[1,2,32,128]{3,2,1,0:T(8,128)} %copy-done.10) | copy-start | bytes 98308
  67.3 24.3 %collective-permute-start.2 = (f32[32,6,1,256]{3,0,2,1:T(8,128)S(1)}, f32[32,6,1,256]{3,0,2,1:T(8,128)S(1)}, u32[]{:S(2)}, u32[]{:S(2)}) collective-permute-start(f32[32,6,1,256]{3,0,2,1:T(8,128)S(1)} %get-tuple-element.11), channel_id=1, source_target_pairs={{0,1},{1,2},{2,3},{3,4},{4,5},{5,6},{6,7},{7,0},{8,9},{9,10},{10,1... | collective-permute-start | bytes 589832 | tf_op jit(solution)/shard_map/ppermute | solution.py:16
  68.4 23.2 %collective-permute-start.3 = (f32[32,6,1,256]{3,0,2,1:T(8,128)S(1)}, f32[32,6,1,256]{3,0,2,1:T(8,128)S(1)}, u32[]{:S(2)}, u32[]{:S(2)}) collective-permute-start(f32[32,6,1,256]{3,0,2,1:T(8,128)S(1)} %get-tuple-element.12), channel_id=1, source_target_pairs={{1,0},{2,1},{3,2},{4,3},{5,4},{6,5},{7,6},{0,7},{9,8},{10,9},{11,1... | collective-permute-start | bytes 589832 | tf_op jit(solution)/shard_map/ppermute | solution.py:17
  72.8 7.4 %copy-start.12 = (f32[1,2,32,128]{3,2,1,0:T(8,128)S(1)}, f32[1,2,32,128]{3,2,1,0:T(8,128)}, u32[]{:S(2)}) copy-start(f32[1,2,32,128]{3,2,1,0:T(8,128)} %get-tuple-element.42) | copy-start | bytes 98308
  72.8 7.4 %copy-start.13 = (f32[1,2,32,128]{3,2,1,0:T(8,128)S(1)}, f32[1,2,32,128]{3,2,1,0:T(8,128)}, u32[]{:S(2)}) copy-start(f32[1,2,32,128]{3,2,1,0:T(8,128)} %get-tuple-element.43) | copy-start | bytes 98308
  81.3 18.1 %all-to-all-start.2 = ((f32[2,1,128,128]{3,0,1,2:T(2,128)}), f32[2,1,128,128]{3,0,1,2:T(2,128)S(1)}, u32[]{:S(2)}, u32[]{:S(2)}) async-start(f32[2,1,128,128]{3,0,1,2:T(2,128)} %copy.67), calls=%async_computation.2 | async-start | bytes 262144 | tf_op jit(solution)/shard_map/all_to_all | solution.py:74
  101.2 14.2 %all-to-all-start.3 = ((f32[2,128,4,128]{3,2,0,1:T(4,128)}), f32[2,128,4,128]{3,2,0,1:T(4,128)S(1)}, u32[]{:S(2)}, u32[]{:S(2)}) async-start(f32[2,128,4,128]{3,2,0,1:T(4,128)} %copy.70), calls=%async_computation.3 | async-start | bytes 1048576 | tf_op jit(solution)/shard_map/all_to_all | solution.py:77
  104.7 3.0 %copy-start.3 = (f32[32,6,16,256]{3,0,2,1:T(8,128)S(1)}, f32[32,6,16,256]{3,0,2,1:T(8,128)}, u32[]{:S(2)}) copy-start(f32[32,6,16,256]{3,0,2,1:T(8,128)} %copy-done.2) | copy-start | bytes 9437188
  117.6 5.6 %copy-start.4 = (f32[32,6,16,256]{3,0,2,1:T(8,128)S(1)}, f32[32,6,16,256]{3,0,2,1:T(8,128)}, u32[]{:S(2)}) copy-start(f32[32,6,16,256]{3,0,2,1:T(8,128)} %copy-done.2) | copy-start | bytes 9437188
  117.6 5.6 %copy-start.15 = (f32[32]{0:T(128)S(1)}, f32[32]{0:T(128)}, u32[]{:S(2)}) copy-start(f32[32]{0:T(128)} %get-tuple-element.15) | copy-start | bytes 388
  117.6 5.6 %copy-start.16 = (f32[32]{0:T(128)S(1)}, f32[32]{0:T(128)}, u32[]{:S(2)}) copy-start(f32[32]{0:T(128)} %get-tuple-element.16) | copy-start | bytes 388
  117.6 5.6 %copy-start.17 = (f32[32]{0:T(128)S(1)}, f32[32]{0:T(128)}, u32[]{:S(2)}) copy-start(f32[32]{0:T(128)} %get-tuple-element.17) | copy-start | bytes 388
  117.6 5.6 %copy-start.18 = (f32[32]{0:T(128)S(1)}, f32[32]{0:T(128)}, u32[]{:S(2)}) copy-start(f32[32]{0:T(128)} %get-tuple-element.18) | copy-start | bytes 388
  117.6 5.6 %copy-start.19 = (f32[32]{0:T(128)S(1)}, f32[32]{0:T(128)}, u32[]{:S(2)}) copy-start(f32[32]{0:T(128)} %get-tuple-element.19) | copy-start | bytes 388
  117.6 5.6 %copy-start.20 = (f32[32]{0:T(128)S(1)}, f32[32]{0:T(128)}, u32[]{:S(2)}) copy-start(f32[32]{0:T(128)} %get-tuple-element.20) | copy-start | bytes 388
  117.6 5.6 %copy-start.21 = (f32[32]{0:T(128)S(1)}, f32[32]{0:T(128)}, u32[]{:S(2)}) copy-start(f32[32]{0:T(128)} %get-tuple-element.21) | copy-start | bytes 388
  117.6 5.6 %copy-start.22 = (f32[32]{0:T(128)S(1)}, f32[32]{0:T(128)}, u32[]{:S(2)}) copy-start(f32[32]{0:T(128)} %get-tuple-element.22) | copy-start | bytes 388
  117.6 5.6 %copy-start.23 = (f32[32]{0:T(128)S(1)}, f32[32]{0:T(128)}, u32[]{:S(2)}) copy-start(f32[32]{0:T(128)} %get-tuple-element.23) | copy-start | bytes 388
  117.6 5.6 %copy-start.24 = (f32[32]{0:T(128)S(1)}, f32[32]{0:T(128)}, u32[]{:S(2)}) copy-start(f32[32]{0:T(128)} %get-tuple-element.24) | copy-start | bytes 388
  117.6 5.6 %copy-start.25 = (f32[32]{0:T(128)S(1)}, f32[32]{0:T(128)}, u32[]{:S(2)}) copy-start(f32[32]{0:T(128)} %get-tuple-element.25) | copy-start | bytes 388
  117.6 5.6 %copy-start.26 = (f32[32]{0:T(128)S(1)}, f32[32]{0:T(128)}, u32[]{:S(2)}) copy-start(f32[32]{0:T(128)} %get-tuple-element.26) | copy-start | bytes 388
  117.7 5.6 %copy-start.27 = (f32[32]{0:T(128)S(1)}, f32[32]{0:T(128)}, u32[]{:S(2)}) copy-start(f32[32]{0:T(128)} %get-tuple-element.27) | copy-start | bytes 388
  117.7 5.6 %copy-start.28 = (f32[32]{0:T(128)S(1)}, f32[32]{0:T(128)}, u32[]{:S(2)}) copy-start(f32[32]{0:T(128)} %get-tuple-element.28) | copy-start | bytes 388
  117.7 5.6 %copy-start.29 = (f32[32]{0:T(128)S(1)}, f32[32]{0:T(128)}, u32[]{:S(2)}) copy-start(f32[32]{0:T(128)} %get-tuple-element.29) | copy-start | bytes 388
  117.7 5.6 %copy-start.30 = (f32[32]{0:T(128)S(1)}, f32[32]{0:T(128)}, u32[]{:S(2)}) copy-start(f32[32]{0:T(128)} %get-tuple-element.30) | copy-start | bytes 388
  117.7 5.6 %copy-start.31 = (f32[32]{0:T(128)S(1)}, f32[32]{0:T(128)}, u32[]{:S(2)}) copy-start(f32[32]{0:T(128)} %get-tuple-element.31) | copy-start | bytes 388
  117.7 5.6 %copy-start.32 = (f32[32]{0:T(128)S(1)}, f32[32]{0:T(128)}, u32[]{:S(2)}) copy-start(f32[32]{0:T(128)} %get-tuple-element.32) | copy-start | bytes 388
  117.7 5.6 %copy-start.33 = (f32[32]{0:T(128)S(1)}, f32[32]{0:T(128)}, u32[]{:S(2)}) copy-start(f32[32]{0:T(128)} %get-tuple-element.33) | copy-start | bytes 388
  117.7 5.6 %copy-start.34 = (f32[32]{0:T(128)S(1)}, f32[32]{0:T(128)}, u32[]{:S(2)}) copy-start(f32[32]{0:T(128)} %get-tuple-element.34) | copy-start | bytes 388
  117.7 5.6 %copy-start.35 = (f32[32]{0:T(128)S(1)}, f32[32]{0:T(128)}, u32[]{:S(2)}) copy-start(f32[32]{0:T(128)} %get-tuple-element.35) | copy-start | bytes 388
  117.7 5.6 %copy-start.36 = (f32[32]{0:T(128)S(1)}, f32[32]{0:T(128)}, u32[]{:S(2)}) copy-start(f32[32]{0:T(128)} %get-tuple-element.36) | copy-start | bytes 388
  117.8 5.6 %copy-start.37 = (f32[32]{0:T(128)S(1)}, f32[32]{0:T(128)}, u32[]{:S(2)}) copy-start(f32[32]{0:T(128)} %get-tuple-element.37) | copy-start | bytes 388
  117.8 5.6 %copy-start.38 = (f32[32]{0:T(128)S(1)}, f32[32]{0:T(128)}, u32[]{:S(2)}) copy-start(f32[32]{0:T(128)} %get-tuple-element.38) | copy-start | bytes 388
  117.8 5.6 %copy-start.39 = (f32[32]{0:T(128)S(1)}, f32[32]{0:T(128)}, u32[]{:S(2)}) copy-start(f32[32]{0:T(128)} %get-tuple-element.39) | copy-start | bytes 388
  117.8 5.6 %copy-start.40 = (f32[32]{0:T(128)S(1)}, f32[32]{0:T(128)}, u32[]{:S(2)}) copy-start(f32[32]{0:T(128)} %get-tuple-element.40) | copy-start | bytes 388
  117.8 5.6 %copy-start.41 = (f32[32]{0:T(128)S(1)}, f32[32]{0:T(128)}, u32[]{:S(2)}) copy-start(f32[32]{0:T(128)} %get-tuple-element.41) | copy-start | bytes 388
  117.8 5.6 %copy-start.42 = (f32[32]{0:T(128)S(1)}, f32[32]{0:T(128)}, u32[]{:S(2)}) copy-start(f32[32]{0:T(128)} %param.9) | copy-start | bytes 388
  (3 other events, 5.4 us)
